TPU v7x, 32 devices: a whole 2x2x4 slice. The times are simulated.
32 devices in a mesh: row: 2 (over x), col: 4 (over z), depth: 4 (over y, core).
Axes of the slice: x: 2, y: 2, z: 4, core: 2. Of those that a mesh axis runs over, the one named last changes fastest.
Arguments:
- x_blocks: bfloat16 [32, 4, 256, 256], P(('row', 'col'), 'depth'), may hold values from -0.25 to 0.25
- x_columns: int32 [32, 4], P(('row', 'col'), 'depth'), may hold values from 0 to 31, as said below
- h_blocks: bfloat16 [32, 4, 256, 256], P(('row', 'col')), may hold values from -6 to 6
- h_columns: int32 [32, 4], P(('row', 'col')), may hold values from 0 to 31, as said below
- p_columns: int32 [32, 4], P(('row', 'col')), may hold values from 0 to 31, as said below
- q_columns: int32 [32, 4], P(('row', 'col')), may hold values from 0 to 31, as said below
Outputs:
- product_p: bfloat16 [32, 4, 256, 256], P(('row', 'col'), 'depth')
- product_q: bfloat16 [32, 4, 256, 256], P(('row', 'col'), 'depth')
Inputs may be any that keep to these rules, and one draw needn't show every extreme that they name: `x_columns`: row i holds 4 distinct block columns (i + o) mod 32 with -2 <= o <= 2. `h_columns`: row i holds 4 distinct block columns (i + o) mod 32 with -2 <= o <= 2. `p_columns`: row i holds 4 distinct block columns (i + o) mod 32 with -4 <= o <= 4. `q_columns`: row i holds 4 distinct block columns (i + o) mod 32 with -6 <= o <= 6.
All inputs are finite; a program needn't handle non-finite values.
Results may differ from a plain program's by a relative error of at most 0.0049.
Values may be sent and summed in bfloat16 or wider, within the bound.
A program may use at most 64 MiB of HBM per device.

v0:
```python
import jax
import jax.numpy as jnp
from jax import lax
from jax.sharding import PartitionSpec as P

REACH = 2


def extended(cells, sides, width):
    for axis, dim in sides:
        count = lax.axis_size(axis)
        head = lax.slice_in_dim(cells, 0, width, axis=dim)
        tail = lax.slice_in_dim(cells, cells.shape[dim] - width, cells.shape[dim], axis=dim)
        cells = jnp.concatenate(
            [
                lax.ppermute(tail, axis, [(i, (i + 1) % count) for i in range(count)]),
                cells,
                lax.ppermute(head, axis, [((i + 1) % count, i) for i in range(count)]),
            ],
            axis=dim,
        )
    return cells


def sparse_product(
    left_blocks, left_columns, rim_blocks, rim_columns, wanted, first_row, width, all_rows
):
    located = jnp.mod(left_columns - first_row + width, all_rows).astype(jnp.int32)
    fetched = rim_blocks[located]
    fetched_columns = rim_columns[located]
    chosen_mask = (fetched_columns[..., None] == wanted[:, None, None, :]).astype(jnp.bfloat16)
    chosen = jnp.einsum(
        "ikmp,ikmbc->ikpbc", chosen_mask, fetched, preferred_element_type=jnp.float32
    ).astype(jnp.bfloat16)
    return jnp.einsum("ikab,ikpbc->ipac", left_blocks, chosen, preferred_element_type=jnp.float32)


def local(x_blocks, x_columns, h_blocks, h_columns, p_columns, q_columns):
    rows_here = x_blocks.shape[0]
    all_rows = rows_here * lax.axis_size(("row", "col"))
    first_row = lax.axis_index(("row", "col")) * rows_here
    depth_index = lax.axis_index("depth")
    depth_count = lax.axis_size("depth")
    slot_share = h_blocks.shape[1] // depth_count
    whole_x, whole_columns = (
        lax.all_gather(x_blocks, "depth", axis=1, tiled=True),
        lax.all_gather(x_columns, "depth", axis=1, tiled=True),
    )
    own_blocks = lax.dynamic_slice_in_dim(h_blocks, depth_index * slot_share, slot_share, 1)
    own_columns = lax.dynamic_slice_in_dim(h_columns, depth_index * slot_share, slot_share, 1)
    rim_blocks, rim_columns = (
        extended(own_blocks, ((("row", "col"), 0),), REACH),
        extended(own_columns, ((("row", "col"), 0),), REACH),
    )
    partial_value = sparse_product(
        whole_x, whole_columns, rim_blocks, rim_columns, p_columns, first_row, REACH, all_rows
    )
    product_p = lax.psum_scatter(partial_value, "depth", scatter_dimension=1, tiled=True).astype(
        jnp.bfloat16
    )
    full_p = lax.all_gather(product_p, "depth", axis=1, tiled=True)
    rim_x, rim_x_columns = (
        extended(x_blocks, ((("row", "col"), 0),), 2 * REACH),
        extended(x_columns, ((("row", "col"), 0),), 2 * REACH),
    )
    q_terms = sparse_product(
        full_p, p_columns, rim_x, rim_x_columns, q_columns, first_row, 2 * REACH, all_rows
    )
    product_q = lax.psum_scatter(q_terms, "depth", scatter_dimension=1, tiled=True).astype(
        jnp.bfloat16
    )
    return (product_p, product_q)


def solution(mesh):
    in_specs = (
        P(("row", "col"), "depth", None, None),
        P(("row", "col"), "depth"),
        P(("row", "col"), None, None, None),
        P(("row", "col"), None),
        P(("row", "col"), None),
        P(("row", "col"), None),
    )
    out_specs = (P(("row", "col"), "depth", None, None), P(("row", "col"), "depth", None, None))
    return jax.shard_map(local, mesh=mesh, in_specs=in_specs, out_specs=out_specs, check_vma=False)
```

profile of v0, /device:TPU:0, one launch (start us, length us, event | category | flops | bytes accessed | tf_op | source)
XLA Modules:
  0.0 247.2 jit_solution(1343871756626057109)
XLA Ops:
  7.2 0.7 all-gather.4.cloned.1.call-update
  8.1 3.1 %collective-permute-start = (s32[2,1]{1,0:T(2,128)S(1)}, s32[2,1]{1,0:T(2,128)S(1)}, u32[]{:S(2)}, u32[]{:S(2)}) collective-permute-start(s32[2,1]{1,0:T(2,128)S(1)} %get-tuple-element.10), channel_id=1, source_target_pairs={{0,4},{4,8},{8,12},{12,16},{16,20},{20,24},{24,28},{28,0},{1,5},{5... | collective-permute-start | bytes 32 | tf_op jit(solution)/shard_map/ppermute | solution.py:16
  11.1 3.0 %collective-permute-start.1 = (s32[2,1]{1,0:T(2,128)S(1)}, s32[2,1]{1,0:T(2,128)S(1)}, u32[]{:S(2)}, u32[]{:S(2)}) collective-permute-start(s32[2,1]{1,0:T(2,128)S(1)} %get-tuple-element.11), channel_id=1, source_target_pairs={{4,0},{8,4},{12,8},{16,12},{20,16},{24,20},{28,24},{0,28},{5,1},{9... | collective-permute-start | bytes 32 | tf_op jit(solution)/shard_map/ppermute | solution.py:18
  14.1 1.1 constant_dynamic-slice_fusion.1
  15.3 4.7 %collective-permute-start.3 = (bf16[2,1,256,256]{3,2,1,0:T(8,128)(2,1)S(1)}, bf16[2,1,256,256]{3,2,1,0:T(8,128)(2,1)S(1)}, u32[]{:S(2)}, u32[]{:S(2)}) collective-permute-start(bf16[2,1,256,256]{3,2,1,0:T(8,128)(2,1)S(1)} %get-tuple-element.9), channel_id=1, source_target_pairs={{4,0},{8,4},{12,8},{16,12},{20,16},{24,20},{28,24},{0,28},{5,1},{9... | collective-permute-start | bytes 786440 | tf_op jit(solution)/shard_map/ppermute | solution.py:18
  20.0 5.3 %all-gather = s32[4,1,4]{2,1,0:T(1,128)S(1)} all-gather(s32[1,1,4]{2,1,0:T(1,128)} %bitcast.54), channel_id=1, replica_groups=mesh['row'=2,'col'=4,'depth'=4] {'depth'}, dimensions={0}, use_global_device_ids=true | all-gather | bytes 80 | tf_op jit(solution)/shard_map/all_gather | solution.py:47
  25.3 0.1 copy.24
  25.5 1.1 constant_dynamic-slice_fusion.2
  26.6 0.6 dynamic-slice
  27.2 0.1 add_reduce_fusion
  27.3 0.7 gather_fusion
  28.2 0.6 collective-permute-done.3
  28.7 0.1 maximum_bitcast_fusion.1
  28.9 0.7 gather_fusion.1
  29.5 2.8 %copy.25 = f32[4,4,256,256]{2,3,1,0:T(8,128)} copy(bf16[4,4,256,256]{3,2,1,0:T(8,128)(2,1)S(1)} %bitcast.51) | data formatting | bytes 6291456 | tf_op jit(solution)/shard_map/convert.6
  32.4 2.5 %all-gather.4.cloned.1.call-done = bf16[4,4,256,256]{3,2,1,0:T(8,128)(2,1)} async-done(((bf16[4,1,256,256]{3,2,1,0:T(8,128)(2,1)}), bf16[4,4,256,256]{3,2,1,0:T(8,128)(2,1)}) %all-gather.4.cloned.1.call-update) | async-done | bytes 2097168 | tf_op jit(solution)/shard_map/all_gather | solution.py:46
  34.9 7.2 %fusion.7 = f32[4,4,256,256]{2,3,1,0:T(8,128)} fusion(f32[4,4,256,256]{2,3,1,0:T(8,128)} %copy.25, f32[4,4,4]{1,2,0:T(4,128)S(1)} %compare_convert_fusion.1, bf16[4,4,256,256]{3,2,1,0:T(8,128)(2,1)} %all-gather.4.cloned.1.call-done), kind=kOutput, calls=%fused_computation.13 | convolution fusion | flops 2155872256 | bytes 10486016 | tf_op jit(solution)/shard_map/ikab,ikpbc->ipac/dot_general | solution.py:35
  42.1 76.0 %all-reduce.4 = bf16[4,4,256,256]{2,3,1,0:T(8,128)(2,1)S(1)} all-reduce(f32[4,4,256,256]{2,3,1,0:T(8,128)} %fusion.7), channel_id=2, replica_groups=mesh['row'=2,'col'=4,'depth'=4] {'depth'}, use_global_device_ids=true, to_apply=%region_0.1.clone | all-reduce | flops 1048576 | bytes 6291456
  118.2 0.7 constant_dynamic-slice_fusion.4
  118.9 1.0 copy.26
  120.0 1.7 collective-permute-start.6
  121.6 3.1 %collective-permute-start.7 = (bf16[4,1,256,256]{3,2,1,0:T(8,128)(2,1)S(1)}, bf16[4,1,256,256]{3,2,1,0:T(8,128)(2,1)S(1)}, u32[]{:S(2)}, u32[]{:S(2)}) collective-permute-start(bf16[4,1,256,256]{3,2,1,0:T(8,128)(2,1)S(1)} %copy-done.1), channel_id=1, source_target_pairs={{4,0},{8,4},{12,8},{16,12},{20,16},{24,20},{28,24},{0,28},{5,1},{9... | collective-permute-start | bytes 1572872 | tf_op jit(solution)/shard_map/ppermute | solution.py:18
  124.7 4.7 %collective-permute-start.5 = (s32[4,1]{0,1:T(1,128)S(1)}, s32[4,1]{0,1:T(1,128)S(1)}, u32[]{:S(2)}, u32[]{:S(2)}) collective-permute-start(s32[4,1]{0,1:T(1,128)S(1)} %copy-done.3), channel_id=1, source_target_pairs={{4,0},{8,4},{12,8},{16,12},{20,16},{24,20},{28,24},{0,28},{5,1},{9... | collective-permute-start | bytes 56 | tf_op jit(solution)/shard_map/ppermute | solution.py:18
  129.8 18.4 %collective-permute-done.4 = s32[4,1]{0,1:T(1,128)S(1)} collective-permute-done((s32[4,1]{0,1:T(1,128)S(1)}, s32[4,1]{0,1:T(1,128)S(1)}, u32[]{:S(2)}, u32[]{:S(2)}) %collective-permute-start.4) | collective-permute-done | bytes 48 | tf_op jit(solution)/shard_map/ppermute | solution.py:16
  148.2 0.7 gather_fusion.2
  149.0 0.2 maximum_bitcast_fusion
  149.2 2.0 gather_fusion.3
  151.2 4.5 %copy.29 = f32[4,4,256,256]{2,3,1,0:T(8,128)} copy(bf16[4,4,256,256]{3,2,1,0:T(8,128)(2,1)} %bitcast.52) | data formatting | bytes 6291456 | tf_op jit(solution)/shard_map/convert.7
  155.7 7.2 %fusion.6 = f32[4,4,256,256]{2,3,1,0:T(8,128)} fusion(f32[4,4,256,256]{2,3,1,0:T(8,128)} %copy.29, f32[4,4,4]{1,2,0:T(4,128)S(1)} %compare_convert_fusion, bf16[4,4,256,256]{3,2,1,0:T(8,128)(2,1)} %all-gather.6.cloned.1.call-done), kind=kOutput, calls=%fused_computation.12 | convolution fusion | flops 2155872256 | bytes 10486016 | tf_op jit(solution)/shard_map/ikab,ikpbc->ipac/dot_general | solution.py:35
  163.0 75.7 %all-reduce.5 = bf16[4,4,256,256]{2,3,1,0:T(8,128)(2,1)S(1)} all-reduce(f32[4,4,256,256]{2,3,1,0:T(8,128)} %fusion.6), channel_id=3, replica_groups=mesh['row'=2,'col'=4,'depth'=4] {'depth'}, use_global_device_ids=true, to_apply=%region_1.2.clone | all-reduce | flops 1048576 | bytes 6291456
  238.7 0.7 dynamic-slice_convert_fusion
  239.4 1.0 copy.30
  (40 shorter events, 1.1 us)
Async XLA Ops:
  7.2 0.8 copy-start
  7.2 19.4 %copy-start.5 = (u32[32]{0:T(128)S(1)}, u32[32]{0:T(128)}, u32[]{:S(2)}) copy-start(u32[32]{0:T(128)} %constant.52) | copy-start | bytes 388
  7.2 27.7 %all-gather.4.cloned.1.call-start = ((), (), s32[]{:S(2)}) async-start(), calls=%async_computation | async-start | bytes 2621440 | tf_op jit(solution)/shard_map/all_gather | solution.py:46
  7.9 147.8 %all-gather.6.cloned.1.call-start = ((), (), s32[]{:S(2)}) async-start(), calls=%async_computation.1 | async-start | bytes 2621440 | tf_op jit(solution)/shard_map/all_gather | solution.py:61
  8.1 19.1 %collective-permute-start = (s32[2,1]{1,0:T(2,128)S(1)}, s32[2,1]{1,0:T(2,128)S(1)}, u32[]{:S(2)}, u32[]{:S(2)}) collective-permute-start(s32[2,1]{1,0:T(2,128)S(1)} %get-tuple-element.10), channel_id=1, source_target_pairs={{0,4},{4,8},{8,12},{12,16},{16,20},{20,24},{24,28},{28,0},{1,5},{5... | collective-permute-start | bytes 32 | tf_op jit(solution)/shard_map/ppermute | solution.py:16
  11.1 16.1 %collective-permute-start.1 = (s32[2,1]{1,0:T(2,128)S(1)}, s32[2,1]{1,0:T(2,128)S(1)}, u32[]{:S(2)}, u32[]{:S(2)}) collective-permute-start(s32[2,1]{1,0:T(2,128)S(1)} %get-tuple-element.11), channel_id=1, source_target_pairs={{4,0},{8,4},{12,8},{16,12},{20,16},{24,20},{28,24},{0,28},{5,1},{9... | collective-permute-start | bytes 32 | tf_op jit(solution)/shard_map/ppermute | solution.py:18
  14.1 13.9 %copy-start.2 = (s32[4,4]{1,0:T(4,128)S(1)}, s32[4,4]{1,0:T(4,128)}, u32[]{:S(2)}) copy-start(s32[4,4]{1,0:T(4,128)} %param.10) | copy-start | bytes 196
  15.2 12.9 %collective-permute-start.2 = (bf16[2,1,256,256]{3,2,1,0:T(8,128)(2,1)S(1)}, bf16[2,1,256,256]{3,2,1,0:T(8,128)(2,1)S(1)}, u32[]{:S(2)}, u32[]{:S(2)}) collective-permute-start(bf16[2,1,256,256]{3,2,1,0:T(8,128)(2,1)S(1)} %get-tuple-element.8), channel_id=1, source_target_pairs={{0,4},{4,8},{8,12},{12,16},{16,20},{20,24},{24,28},{28,0},{1,5},{5... | collective-permute-start | bytes 786440 | tf_op jit(solution)/shard_map/ppermute | solution.py:16
  15.3 13.4 %collective-permute-start.3 = (bf16[2,1,256,256]{3,2,1,0:T(8,128)(2,1)S(1)}, bf16[2,1,256,256]{3,2,1,0:T(8,128)(2,1)S(1)}, u32[]{:S(2)}, u32[]{:S(2)}) collective-permute-start(bf16[2,1,256,256]{3,2,1,0:T(8,128)(2,1)S(1)} %get-tuple-element.9), channel_id=1, source_target_pairs={{4,0},{8,4},{12,8},{16,12},{20,16},{24,20},{28,24},{0,28},{5,1},{9... | collective-permute-start | bytes 786440 | tf_op jit(solution)/shard_map/ppermute | solution.py:18
  118.1 1.8 copy-start.1
  118.2 6.6 %copy-start.3 = (s32[4,1]{0,1:T(1,128)S(1)}, s32[4,1]{0,1:T(1,128)}, u32[]{:S(2)}) copy-start(s32[4,1]{0,1:T(1,128)} %param.7) | copy-start | bytes 52
  118.9 30.0 %copy-start.4 = (s32[4,4]{1,0:T(4,128)S(1)}, s32[4,4]{1,0:T(4,128)}, u32[]{:S(2)}) copy-start(s32[4,4]{1,0:T(4,128)} %param.11) | copy-start | bytes 196
  120.0 29.1 %collective-permute-start.6 = (bf16[4,1,256,256]{3,2,1,0:T(8,128)(2,1)S(1)}, bf16[4,1,256,256]{3,2,1,0:T(8,128)(2,1)S(1)}, u32[]{:S(2)}, u32[]{:S(2)}) collective-permute-start(bf16[4,1,256,256]{3,2,1,0:T(8,128)(2,1)S(1)} %copy-done.1), channel_id=1, source_target_pairs={{0,4},{4,8},{8,12},{12,16},{16,20},{20,24},{24,28},{28,0},{1,5},{5... | collective-permute-start | bytes 1572872 | tf_op jit(solution)/shard_map/ppermute | solution.py:16
  121.6 27.4 %collective-permute-start.7 = (bf16[4,1,256,256]{3,2,1,0:T(8,128)(2,1)S(1)}, bf16[4,1,256,256]{3,2,1,0:T(8,128)(2,1)S(1)}, u32[]{:S(2)}, u32[]{:S(2)}) collective-permute-start(bf16[4,1,256,256]{3,2,1,0:T(8,128)(2,1)S(1)} %copy-done.1), channel_id=1, source_target_pairs={{4,0},{8,4},{12,8},{16,12},{20,16},{24,20},{28,24},{0,28},{5,1},{9... | collective-permute-start | bytes 1572872 | tf_op jit(solution)/shard_map/ppermute | solution.py:18
  124.7 23.4 %collective-permute-start.4 = (s32[4,1]{0,1:T(1,128)S(1)}, s32[4,1]{0,1:T(1,128)S(1)}, u32[]{:S(2)}, u32[]{:S(2)}) collective-permute-start(s32[4,1]{0,1:T(1,128)S(1)} %copy-done.3), channel_id=1, source_target_pairs={{0,4},{4,8},{8,12},{12,16},{16,20},{20,24},{24,28},{28,0},{1,5},{5... | collective-permute-start | bytes 56 | tf_op jit(solution)/shard_map/ppermute | solution.py:16
  124.7 23.4 %collective-permute-start.5 = (s32[4,1]{0,1:T(1,128)S(1)}, s32[4,1]{0,1:T(1,128)S(1)}, u32[]{:S(2)}, u32[]{:S(2)}) collective-permute-start(s32[4,1]{0,1:T(1,128)S(1)} %copy-done.3), channel_id=1, source_target_pairs={{4,0},{8,4},{12,8},{16,12},{20,16},{24,20},{28,24},{0,28},{5,1},{9... | collective-permute-start | bytes 56 | tf_op jit(solution)/shard_map/ppermute | solution.py:18
Sparse Core Ops, SparseCore 0:
  9.6 25.2 all-gather.3
  120.1 23.6 all-gather.5
where the time goes:
time: 248 us; the launch traced here: 247 us
  blocking collectives  157 us (63%)
  waiting for transfers between devices  22.2 us (9%)
  starting transfers between devices  20.4 us (8%)
  local copies, waits for them, and re-layouts  18.2 us (7%)
  matrix products  14.4 us (6%)
  between operations  14.2 us (6%)
    unnamed x2, blocking collectives  152 us
    ppermute x4, waiting for transfers between devices, extended(): lax.ppermute(tail, axis, [(i, (i + 1) % count) for i in range(count)])  18.4 us
    ppermute x4, starting transfers between devices, extended(): lax.ppermute(head, axis, [((i + 1) % count, i) for i in range(count)])  15.5 us
    dot_general x2, matrix products, sparse_product(): jnp.einsum('ikab,ikpbc->ipac', left_blocks, chosen, preferred_element_typ...  14.4 us
    another operation x2, local copies, waits for them, and re-layouts  7.32 us
    all_gather x1, blocking collectives, local(): lax.all_gather(x_columns, 'depth', axis=1, tiled=True)  5.32 us
  transfers between devices with their start and end apart: 10, of which 3 were waited for; matrix products, arithmetic and copies ran while one was open for 6% of the time, Pallas kernels for 0%

commit v1 on v0

v1 whole, which is shorter than its diff:
```python
import functools

import jax
import jax.numpy as jnp
from jax import lax
from jax.experimental import pallas as pl
from jax.experimental.pallas import tpu as pltpu
from jax.sharding import PartitionSpec as P

REACH = 2
MESH = pl.DeviceIdType.MESH


def kernel(
    sizes, x_ref, h_ref, meta_ref, p_cols, q_cols,
    out_p, out_q,
    xb, xo, hb, pb, qb, meta_v, meta_s, send_sem, recv_sem, local_sem,
):
    rows_n, cols_n, rows_here, slots, block = sizes
    groups = rows_n * cols_n
    all_rows = groups * rows_here
    half_w = block // 2
    own_rows = rows_here // 2
    wide = 2 * REACH
    group = lax.axis_index("row") * cols_n + lax.axis_index("col")
    d = lax.axis_index("depth")
    y = d // 2
    c = lax.rem(d, 2)
    first_row = group * rows_here

    def at(step, depth):
        g = lax.rem(group + step + groups, groups)
        return (g // cols_n, lax.rem(g, cols_n), depth)

    def other(dy, dc):
        yy = lax.rem(y + dy, 2)
        cc = lax.rem(c + dc, 2)
        return yy, cc, yy * 2 + cc

    mates = [(0, 1), (1, 0), (1, 1)]
    peers = [(0, dy, dc) for dy, dc in mates]
    peers += [(s, dy, dc) for s in (1, -1) for dy in (0, 1) for dc in (0, 1)]

    barrier = pltpu.get_barrier_semaphore()
    for s, dy, dc in peers:
        pl.semaphore_signal(
            barrier, inc=1, device_id=at(s, other(dy, dc)[2]), device_id_type=MESH
        )
    pl.semaphore_wait(barrier, len(peers))

    counts = {"remote": 0, "local": 0}
    started = []

    def send(src, dst, to):
        n = counts["remote"]
        counts["remote"] = n + 1
        copy = pltpu.make_async_remote_copy(
            src_ref=src, dst_ref=dst, send_sem=send_sem.at[n], recv_sem=recv_sem.at[n],
            device_id=to, device_id_type=MESH,
        )
        copy.start()
        started.append(copy)
        return copy

    def move(src, dst):
        n = counts["local"]
        counts["local"] = n + 1
        copy = pltpu.make_async_copy(src, dst, local_sem.at[n])
        copy.start()
        return copy

    def side(which):
        return pl.ds(pl.multiple_of(which * half_w, half_w), half_w)

    here = pl.ds(wide, rows_here)
    over = at(0, other(1, 0)[2])
    partner = at(0, other(0, 1)[2])

    metas = [
        send(meta_ref, meta_v.at[(1 - s) * slots + d], at(s, other(dy, dc)[2]))
        for s, dy, dc in peers
    ]
    own_meta = move(meta_ref, meta_v.at[slots + d])

    y_near = send(x_ref.at[:, 0, :, side(1 - y)], xb.at[here, c, y], over)
    local_x = move(x_ref.at[:, 0, :, side(y)], xb.at[here, c, y])

    mine = pl.ds(c * (slots // 2), slots // 2)
    h_up = send(
        h_ref.at[pl.ds(rows_here - REACH, REACH), mine, :, side(y)],
        hb.at[pl.ds(0, REACH), mine], at(1, d),
    )
    h_down = send(
        h_ref.at[pl.ds(0, REACH), mine, :, side(y)],
        hb.at[pl.ds(REACH + rows_here, REACH), mine], at(-1, d),
    )
    y_far = send(x_ref.at[:, 0, :, side(y)], xo.at[:, c, y], over)
    local_o = move(x_ref.at[:, 0, :, side(1 - y)], xo.at[:, c, y])
    local_h = move(h_ref.at[:, :, :, side(y)], hb.at[pl.ds(REACH, rows_here)])
    d2d = [
        send(x_ref.at[:, 0, :, side(y)], xb.at[here, c, y], partner),
        send(x_ref.at[:, 0, :, side(1 - y)], xo.at[:, c, y], partner),
    ]
    zeros = jnp.zeros((block, half_w), hb.dtype)
    hb[rows_here + 2 * REACH, 0] = zeros
    xb[rows_here + 2 * wide, 0, 0] = zeros

    local_x.wait()
    y_near.wait_recv()
    rim = []
    for step in range(rows_here):
        down = rows_here - 1 - step
        rim.append((send(xb.at[wide + down, c], xb.at[down, c], at(1, d)), down))
        rim.append(
            (
                send(xb.at[wide + step, c], xb.at[wide + rows_here + step, c], at(-1, d)),
                wide + rows_here + step,
            )
        )
    d2d.append(send(xb.at[here, c, 1 - y], xb.at[here, c, 1 - y], partner))
    y_far.wait_recv()
    d2d.append(send(xo.at[:, c, 1 - y], xo.at[:, c, 1 - y], partner))
    own_meta.wait()
    for copy in metas:
        copy.wait_recv()
    to_smem = move(meta_v, meta_s)
    h_up.wait_recv()
    ref = hb.at[pl.ds(0, REACH), mine]
    d2d.append(send(ref, ref, partner))
    h_down.wait_recv()
    ref = hb.at[pl.ds(REACH + rows_here, REACH), mine]
    d2d.append(send(ref, ref, partner))
    to_smem.wait()
    local_o.wait()
    local_h.wait()
    for copy in d2d:
        copy.wait_recv()

    p_moves = []
    for ii in range(own_rows):
        i = c * own_rows + ii

        def p_block(p, carry, i=i, ii=ii):
            wanted = p_cols[i, p]
            total = jnp.zeros((block, half_w), jnp.float32)
            for k in range(slots):
                column = meta_s[slots + k, i, slots]
                r = lax.rem(column - first_row + REACH + all_rows, all_rows)
                r = jnp.clip(r, 0, rows_here + 2 * REACH - 1)
                part = r + rows_here - REACH
                s = part // rows_here
                row = lax.rem(part, rows_here)
                pick_r = jnp.int32(rows_here + 2 * REACH)
                pick_m = jnp.int32(0)
                for m in range(slots):
                    hit = meta_s[s * slots, row, m] == wanted
                    pick_r = jnp.where(hit, r, pick_r)
                    pick_m = jnp.where(hit, m, pick_m)
                near = xb[wide + i, k % 2, k // 2]
                far = xo[i, k % 2, k // 2]
                left = jnp.concatenate(
                    [jnp.where(y == 0, near, far), jnp.where(y == 0, far, near)], axis=1
                )
                total += jnp.dot(left, hb[pick_r, pick_m], preferred_element_type=jnp.float32)
            pb[y, ii, p] = total.astype(pb.dtype)
            return carry

        lax.fori_loop(0, slots, p_block, 0)
        p_moves.append(send(pb.at[y, ii], pb.at[y, ii], over))

    rim_d2d = []
    for copy, row in rim:
        copy.wait_recv()
        rim_d2d.append(send(xb.at[row, c], xb.at[row, c], partner))
    for copy in p_moves:
        copy.wait_recv()

    where = pl.ds(c * own_rows, own_rows)
    outs = []
    moves = []
    for half in range(2):
        cut = pl.ds(half * half_w, half_w)
        outs.append(
            send(pb.at[half, :, other(0, 1)[2]], out_p.at[where, 0, :, cut], partner)
        )
        moves.append(move(pb.at[half, :, d], out_p.at[where, 0, :, cut]))
    for copy in rim_d2d:
        copy.wait_recv()

    for ii in range(own_rows):
        i = c * own_rows + ii

        def q_block(q, carry, i=i, ii=ii):
            wanted = q_cols[i, q]
            total = jnp.zeros((block, half_w), jnp.float32)
            for p in range(slots):
                r = lax.rem(p_cols[i, p] - first_row + wide + all_rows, all_rows)
                r = jnp.clip(r, 0, rows_here + 2 * wide - 1)
                s = r // rows_here
                row = lax.rem(r, rows_here)
                pick_r = jnp.int32(rows_here + 2 * wide)
                pick_c = jnp.int32(0)
                pick_y = jnp.int32(0)
                for m in range(slots):
                    hit = meta_s[s * slots + m, row, slots] == wanted
                    pick_r = jnp.where(hit, r, pick_r)
                    pick_c = jnp.where(hit, m % 2, pick_c)
                    pick_y = jnp.where(hit, m // 2, pick_y)
                left = jnp.concatenate([pb[0, ii, p], pb[1, ii, p]], axis=1)
                total += jnp.dot(
                    left, xb[pick_r, pick_c, pick_y], preferred_element_type=jnp.float32
                )
            qb[ii, q] = total.astype(qb.dtype)
            return carry

        lax.fori_loop(0, slots, q_block, 0)
        place = pl.ds(c * own_rows + ii, 1)
        for dy, dc in ((1, 0), (1, 1), (0, 1)):
            to = other(dy, dc)[2]
            outs.append(
                send(qb.at[pl.ds(ii, 1), to], out_q.at[place, 0, :, side(y)], at(0, to))
            )
        moves.append(move(qb.at[pl.ds(ii, 1), d], out_q.at[place, 0, :, side(y)]))

    for copy in outs:
        copy.wait_recv()
    for copy in moves:
        copy.wait()
    for copy in started:
        copy.wait_send()


def local(sizes, x_blocks, x_columns, h_blocks, h_columns, p_columns, q_columns):
    rows_n, cols_n = sizes
    rows_here, _, block, _ = x_blocks.shape
    slots = h_blocks.shape[1]
    dtype = x_blocks.dtype
    meta = jnp.concatenate([h_columns, x_columns], axis=1)
    meta = jnp.pad(meta, ((0, 8 - rows_here), (0, 128 - meta.shape[1])))
    half_w = block // 2
    any_space = pl.BlockSpec(memory_space=pl.ANY)
    smem = pl.BlockSpec(memory_space=pltpu.SMEM)
    vmem = pl.BlockSpec(memory_space=pltpu.VMEM)
    out = jax.ShapeDtypeStruct(x_blocks.shape, dtype)
    copies = 64
    return pl.pallas_call(
        functools.partial(kernel, (rows_n, cols_n, rows_here, slots, block)),
        out_shape=(out, out),
        in_specs=[any_space, any_space, vmem, smem, smem],
        out_specs=(any_space, any_space),
        scratch_shapes=[
            pltpu.VMEM((rows_here + 4 * REACH + 1, 2, slots // 2, block, half_w), dtype),
            pltpu.VMEM((rows_here, 2, slots // 2, block, half_w), dtype),
            pltpu.VMEM((rows_here + 2 * REACH + 1, slots, block, half_w), dtype),
            pltpu.VMEM((2, rows_here // 2, slots, block, half_w), dtype),
            pltpu.VMEM((rows_here // 2, slots, block, half_w), dtype),
            pltpu.VMEM((3 * slots, 8, 128), jnp.int32),
            pltpu.SMEM((3 * slots, 8, 128), jnp.int32),
            pltpu.SemaphoreType.DMA((copies,)),
            pltpu.SemaphoreType.DMA((copies,)),
            pltpu.SemaphoreType.DMA((16,)),
        ],
        compiler_params=pltpu.CompilerParams(
            collective_id=0, has_side_effects=True, vmem_limit_bytes=48 * 2**20
        ),
    )(x_blocks, h_blocks, meta, p_columns, q_columns)


def solution(mesh):
    in_specs = (
        P(("row", "col"), "depth", None, None),
        P(("row", "col"), "depth"),
        P(("row", "col"), None, None, None),
        P(("row", "col"), None),
        P(("row", "col"), None),
        P(("row", "col"), None),
    )
    out_specs = (P(("row", "col"), "depth", None, None), P(("row", "col"), "depth", None, None))
    sizes = (mesh.shape["row"], mesh.shape["col"])
    return jax.shard_map(
        functools.partial(local, sizes), mesh=mesh, in_specs=in_specs, out_specs=out_specs,
        check_vma=False,
    )
```

time: 248 us -> 60.6 us (0.24)
  blocking collectives: 157 us -> 0 us
  Pallas kernels: 0 us -> 52.3 us
  waiting for transfers between devices: 22.2 us -> 0 us
  starting transfers between devices: 20.4 us -> 0 us
  matrix products: 14.4 us -> 0 us
  between operations: 14.2 us -> 0.64 us
  local copies, waits for them, and re-layouts: 18.2 us -> 6.33 us
    unnamed x2 -> x0, blocking collectives: 152 us -> none
    pallas_call x0 -> x1, Pallas kernels: none -> 52.3 us  [local(): pl.pallas_call(functools.partial(kernel, (rows_n, cols_n, rows_here, slot...]
    ppermute x8 -> x0, starting transfers between devices: 20.3 us -> none  [the longest x4 15.5 us: extended(): lax.ppermute(head, axis, [((i + 1) % count, i) for i in range(count)])]
    ppermute x8 -> x0, waiting for transfers between devices: 18.9 us -> none  [the longest x4 18.4 us: extended(): lax.ppermute(tail, axis, [(i, (i + 1) % count) for i in range(count)])]
    dot_general x2 -> x0, matrix products: 14.4 us -> none  [sparse_product(): jnp.einsum('ikab,ikpbc->ipac', left_blocks, chosen, preferred_element_typ...]
    another operation x2 -> x0, local copies, waits for them, and re-layouts: 7.32 us -> none
    all_gather x1 -> x0, blocking collectives: 5.32 us -> none  [local(): lax.all_gather(x_columns, 'depth', axis=1, tiled=True)]
    gather x4 -> x0, local copies, waits for them, and re-layouts: 4.01 us -> none  [the longest x2 2.7 us: sparse_product(): fetched = rim_blocks[located]]
  transfers between devices with their start and end apart: 10 -> 0, of which waited for: 3 -> 0; matrix products, arithmetic and copies ran while one was open for 6% -> 0% of each run, Pallas kernels for 0% -> 0%
where the time goes in v1:
time: 60.6 us; the launch traced here: 60 us
  Pallas kernels  52.3 us (86%)
  local copies, waits for them, and re-layouts  6.33 us (10%)
  other arithmetic  0.75 us (1%)
  between operations  0.64 us (1%)
    pallas_call x1, Pallas kernels, local(): pl.pallas_call(functools.partial(kernel, (rows_n, cols_n, rows_here, slot...  52.3 us
    unnamed x11, local copies, waits for them, and re-layouts  6.32 us

profile of v1, /device:TPU:0, one launch (start us, length us, event | category | flops | bytes accessed | tf_op | source)
XLA Modules:
  0.0 60.0 jit_solution(14798352537402011192)
XLA Ops:
  0.6 0.7 %copy.8 = s32[4,1]{1,0:T(4,128)S(1)} copy(s32[4,1]{0,1:T(1,128)} %param.7) | data formatting | bytes 32 | tf_op args[1]
  1.4 0.8 %pad_add_fusion = s32[4,5]{1,0:T(4,128)S(1)} fusion(s32[4,1]{1,0:T(4,128)S(1)} %copy.8, s32[4,4]{1,0:T(4,128)} %param.9), kind=kLoop, calls=%fused_computation | loop fusion | flops 20 | bytes 160 | tf_op jit(solution)/shard_map/concatenate | solution.py:238
  2.1 0.0 copy-start
  2.1 1.6 %copy-done = bf16[4,4,256,256]{3,2,1,0:T(8,128)(2,1)S(1)} copy-done((bf16[4,4,256,256]{3,2,1,0:T(8,128)(2,1)S(1)}, bf16[4,4,256,256]{3,2,1,0:T(8,128)(2,1)}, u32[]{:S(2)}) %copy-start) | copy-done | bytes 2097176
  3.7 0.0 copy-start.1
  3.7 1.0 %copy-done.1 = bf16[4,1,256,256]{3,2,1,0:T(8,128)(2,1)S(1)} copy-done((bf16[4,1,256,256]{3,2,1,0:T(8,128)(2,1)S(1)}, bf16[4,1,256,256]{3,2,1,0:T(8,128)(2,1)}, u32[]{:S(2)}) %copy-start.1) | copy-done | bytes 524312
  4.8 0.0 copy-start.2
  4.8 0.7 %copy-done.2 = s32[4,4]{1,0:T(4,128)S(1)} copy-done((s32[4,4]{1,0:T(4,128)S(1)}, s32[4,4]{1,0:T(4,128)}, u32[]{:S(2)}) %copy-start.2) | copy-done | bytes 88
  5.5 0.0 copy-start.3
  5.5 0.7 %copy-done.3 = s32[4,4]{1,0:T(4,128)S(1)} copy-done((s32[4,4]{1,0:T(4,128)S(1)}, s32[4,4]{1,0:T(4,128)}, u32[]{:S(2)}) %copy-start.3) | copy-done | bytes 88
  6.1 52.3 %shard_map.77 = (bf16[4,1,256,256]{3,2,1,0:T(8,128)(2,1)S(1)}, bf16[4,1,256,256]{3,2,1,0:T(8,128)(2,1)S(1)}) custom-call(bf16[4,1,256,256]{3,2,1,0:T(8,128)(2,1)S(1)} %copy-done.1, bf16[4,4,256,256]{3,2,1,0:T(8,128)(2,1)S(1)} %copy-done, s32[8,128]{1,0:T(8,128)S(1)} %pad.4.meta_ref, s32[4,4]{1,0:T(4,128)S(1)} %copy-done.2, s32[4,4]{1,0:T(4,128)S(1)} %copy-done.3), custom_call_target="tpu_custom_call" | custom-call | tf_op jit(solution)/shard_map/pallas_call | solution.py:246
  58.4 0.8 %copy.11 = bf16[4,1,256,256]{3,2,1,0:T(8,128)(2,1)} copy(bf16[4,1,256,256]{3,2,1,0:T(8,128)(2,1)S(1)} %get-tuple-element.4) | data formatting | bytes 1048576
  59.2 0.8 %copy.12 = bf16[4,1,256,256]{3,2,1,0:T(8,128)(2,1)} copy(bf16[4,1,256,256]{3,2,1,0:T(8,128)(2,1)S(1)} %get-tuple-element.5) | data formatting | bytes 1048576
  (1 shorter events, 0.0 us)
Async XLA Ops:
  2.1 1.6 %copy-start = (bf16[4,4,256,256]{3,2,1,0:T(8,128)(2,1)S(1)}, bf16[4,4,256,256]{3,2,1,0:T(8,128)(2,1)}, u32[]{:S(2)}) copy-start(bf16[4,4,256,256]{3,2,1,0:T(8,128)(2,1)} %h_ref.1) | copy-start | bytes 6291460
  3.7 1.0 %copy-start.1 = (bf16[4,1,256,256]{3,2,1,0:T(8,128)(2,1)S(1)}, bf16[4,1,256,256]{3,2,1,0:T(8,128)(2,1)}, u32[]{:S(2)}) copy-start(bf16[4,1,256,256]{3,2,1,0:T(8,128)(2,1)} %x_ref.1) | copy-start | bytes 1572868
  4.8 0.7 %copy-start.2 = (s32[4,4]{1,0:T(4,128)S(1)}, s32[4,4]{1,0:T(4,128)}, u32[]{:S(2)}) copy-start(s32[4,4]{1,0:T(4,128)} %p_cols.1) | copy-start | bytes 196
  5.5 0.7 %copy-start.3 = (s32[4,4]{1,0:T(4,128)S(1)}, s32[4,4]{1,0:T(4,128)}, u32[]{:S(2)}) copy-start(s32[4,4]{1,0:T(4,128)} %q_cols.1) | copy-start | bytes 196

commit v2 on v1

--- a/solution.py
+++ b/solution.py
@@ -12,9 +12,10 @@
 
 
 def kernel(
-    sizes, x_ref, h_ref, meta_ref, p_cols, q_cols,
+    sizes, x_ref, h_ref, xc_ref, hc_ref, pc_ref, qc_ref,
     out_p, out_q,
-    xb, xo, hb, pb, qb, meta_v, meta_s, send_sem, recv_sem, local_sem,
+    xb, xt, xo, hb, pb, qb, qacc, xc_v, hc_v, x_cols, h_cols, p_cols, q_cols,
+    send_sem, recv_sem, local_sem,
 ):
     rows_n, cols_n, rows_here, slots, block = sizes
     groups = rows_n * cols_n
@@ -72,15 +73,21 @@
     def side(which):
         return pl.ds(pl.multiple_of(which * half_w, half_w), half_w)
 
-    here = pl.ds(wide, rows_here)
+    here = pl.ds(wide - 1, rows_here)
+    xb_zero = rows_here + 2 * wide - 2
+    hb_zero = rows_here + 2 * REACH
     over = at(0, other(1, 0)[2])
     partner = at(0, other(0, 1)[2])
 
     metas = [
-        send(meta_ref, meta_v.at[(1 - s) * slots + d], at(s, other(dy, dc)[2]))
+        send(xc_ref, xc_v.at[(1 - s) * slots + d], at(s, other(dy, dc)[2]))
         for s, dy, dc in peers
     ]
-    own_meta = move(meta_ref, meta_v.at[slots + d])
+    metas += [send(hc_ref, hc_v.at[1 - s], at(s, d)) for s in (1, -1)]
+    own_meta = [
+        move(xc_ref, xc_v.at[slots + d]), move(hc_ref, hc_v.at[1]),
+        move(pc_ref, p_cols), move(qc_ref, q_cols),
+    ]
 
     y_near = send(x_ref.at[:, 0, :, side(1 - y)], xb.at[here, c, y], over)
     local_x = move(x_ref.at[:, 0, :, side(y)], xb.at[here, c, y])
@@ -102,35 +109,39 @@
         send(x_ref.at[:, 0, :, side(1 - y)], xo.at[:, c, y], partner),
     ]
     zeros = jnp.zeros((block, half_w), hb.dtype)
-    hb[rows_here + 2 * REACH, 0] = zeros
-    xb[rows_here + 2 * wide, 0, 0] = zeros
+    hb[hb_zero, 0] = zeros
+    xb[xb_zero, 0, 0] = zeros
+    xt[3, 0] = zeros
 
     local_x.wait()
     y_near.wait_recv()
     rim = []
-    for step in range(rows_here):
+    for step in range(rows_here - 1):
         down = rows_here - 1 - step
-        rim.append((send(xb.at[wide + down, c], xb.at[down, c], at(1, d)), down))
-        rim.append(
-            (
-                send(xb.at[wide + step, c], xb.at[wide + rows_here + step, c], at(-1, d)),
-                wide + rows_here + step,
-            )
-        )
+        for row, place, to in (
+            (down, down, 1), (step, wide + rows_here + step, -1)
+        ):
+            rim.append((send(xb.at[wide - 1 + row, c], xb.at[place - 1, c], at(to, d)), place - 1))
+    late = [
+        send(xb.at[wide - 1, c], xt.at[2 * c], at(1, d)),
+        send(xb.at[wide - 1 + rows_here - 1, c], xt.at[2 - c], at(-1, d)),
+    ]
     d2d.append(send(xb.at[here, c, 1 - y], xb.at[here, c, 1 - y], partner))
     y_far.wait_recv()
     d2d.append(send(xo.at[:, c, 1 - y], xo.at[:, c, 1 - y], partner))
-    own_meta.wait()
+    for copy in own_meta:
+        copy.wait()
     for copy in metas:
         copy.wait_recv()
-    to_smem = move(meta_v, meta_s)
+    to_smem = [move(xc_v, x_cols), move(hc_v, h_cols)]
     h_up.wait_recv()
     ref = hb.at[pl.ds(0, REACH), mine]
     d2d.append(send(ref, ref, partner))
     h_down.wait_recv()
     ref = hb.at[pl.ds(REACH + rows_here, REACH), mine]
     d2d.append(send(ref, ref, partner))
-    to_smem.wait()
+    for copy in to_smem:
+        copy.wait()
     local_o.wait()
     local_h.wait()
     for copy in d2d:
@@ -144,19 +155,19 @@
             wanted = p_cols[i, p]
             total = jnp.zeros((block, half_w), jnp.float32)
             for k in range(slots):
-                column = meta_s[slots + k, i, slots]
+                column = x_cols[slots + k, 0, i]
                 r = lax.rem(column - first_row + REACH + all_rows, all_rows)
                 r = jnp.clip(r, 0, rows_here + 2 * REACH - 1)
                 part = r + rows_here - REACH
                 s = part // rows_here
                 row = lax.rem(part, rows_here)
-                pick_r = jnp.int32(rows_here + 2 * REACH)
+                pick_r = jnp.int32(hb_zero)
                 pick_m = jnp.int32(0)
                 for m in range(slots):
-                    hit = meta_s[s * slots, row, m] == wanted
+                    hit = h_cols[s, row, m] == wanted
                     pick_r = jnp.where(hit, r, pick_r)
                     pick_m = jnp.where(hit, m, pick_m)
-                near = xb[wide + i, k % 2, k // 2]
+                near = xb[wide - 1 + i, k % 2, k // 2]
                 far = xo[i, k % 2, k // 2]
                 left = jnp.concatenate(
                     [jnp.where(y == 0, near, far), jnp.where(y == 0, far, near)], axis=1
@@ -187,40 +198,84 @@
     for copy in rim_d2d:
         copy.wait_recv()
 
-    for ii in range(own_rows):
+    def window(i, p):
+        r = lax.rem(p_cols[i, p] - first_row + wide + all_rows, all_rows)
+        return jnp.clip(r, 0, last_row)
+
+    def hand_on(ii, q):
+        place = pl.ds(c * own_rows + ii, 1)
+        dst = out_q.at[place, 0, :, side(y)]
+        outs.append(send(qb.at[pl.ds(ii, 1), q], dst, at(0, q)))
+
+    def keep(ii):
+        place = pl.ds(c * own_rows + ii, 1)
+        moves.append(move(qb.at[pl.ds(ii, 1), d], out_q.at[place, 0, :, side(y)]))
+
+    last_row = rows_here + 2 * wide - 1
+    order = ((1, 0), (1, 1), (0, 1))
+    for turn in range(own_rows):
+        ii = (1 - c) * (own_rows - 1 - turn) + c * turn
         i = c * own_rows + ii
 
-        def q_block(q, carry, i=i, ii=ii):
+        def q_block(q, carry, i=i, ii=ii, turn=turn):
             wanted = q_cols[i, q]
             total = jnp.zeros((block, half_w), jnp.float32)
             for p in range(slots):
-                r = lax.rem(p_cols[i, p] - first_row + wide + all_rows, all_rows)
-                r = jnp.clip(r, 0, rows_here + 2 * wide - 1)
+                r = window(i, p)
                 s = r // rows_here
                 row = lax.rem(r, rows_here)
-                pick_r = jnp.int32(rows_here + 2 * wide)
+                inner = jnp.logical_and(r > 0, r < last_row)
+                pick_r = jnp.int32(xb_zero)
                 pick_c = jnp.int32(0)
                 pick_y = jnp.int32(0)
                 for m in range(slots):
-                    hit = meta_s[s * slots + m, row, slots] == wanted
-                    pick_r = jnp.where(hit, r, pick_r)
+                    hit = jnp.logical_and(inner, x_cols[s * slots + m, 0, row] == wanted)
+                    pick_r = jnp.where(hit, r - 1, pick_r)
                     pick_c = jnp.where(hit, m % 2, pick_c)
                     pick_y = jnp.where(hit, m // 2, pick_y)
                 left = jnp.concatenate([pb[0, ii, p], pb[1, ii, p]], axis=1)
                 total += jnp.dot(
                     left, xb[pick_r, pick_c, pick_y], preferred_element_type=jnp.float32
                 )
-            qb[ii, q] = total.astype(qb.dtype)
+            if turn < own_rows - 1:
+                qb[ii, q] = total.astype(qb.dtype)
+            else:
+                qacc[q] = total
             return carry
 
         lax.fori_loop(0, slots, q_block, 0)
-        place = pl.ds(c * own_rows + ii, 1)
-        for dy, dc in ((1, 0), (1, 1), (0, 1)):
-            to = other(dy, dc)[2]
-            outs.append(
-                send(qb.at[pl.ds(ii, 1), to], out_q.at[place, 0, :, side(y)], at(0, to))
-            )
-        moves.append(move(qb.at[pl.ds(ii, 1), d], out_q.at[place, 0, :, side(y)]))
+        if turn < own_rows - 1:
+            for dy, dc in order:
+                hand_on(ii, other(dy, dc)[2])
+            keep(ii)
+
+    final = c * last_row
+    pick_p = jnp.int32(0)
+    some = jnp.int32(0)
+    for p in range(slots):
+        hit = window(i, p) == final
+        pick_p = jnp.where(hit, p, pick_p)
+        some = jnp.where(hit, 1, some)
+    left = jnp.concatenate([pb[0, ii, pick_p], pb[1, ii, pick_p]], axis=1)
+    for copy in late:
+        copy.wait_recv()
+    last = send(xt.at[2], xt.at[c], partner)
+    last.wait_recv()
+    for dy, dc in order + ((0, 0),):
+        q = other(dy, dc)[2]
+        wanted = q_cols[i, q]
+        pick_c = jnp.int32(3)
+        pick_y = jnp.int32(0)
+        for m in range(slots):
+            column = x_cols[2 * c * slots + m, 0, c * (rows_here - 1)]
+            hit = jnp.logical_and(some == 1, column == wanted)
+            pick_c = jnp.where(hit, m % 2, pick_c)
+            pick_y = jnp.where(hit, m // 2, pick_y)
+        total = qacc[q] + jnp.dot(left, xt[pick_c, pick_y], preferred_element_type=jnp.float32)
+        qb[ii, q] = total.astype(qb.dtype)
+        if (dy, dc) != (0, 0):
+            hand_on(ii, q)
+    keep(ii)
 
     for copy in outs:
         copy.wait_recv()
@@ -235,35 +290,38 @@
     rows_here, _, block, _ = x_blocks.shape
     slots = h_blocks.shape[1]
     dtype = x_blocks.dtype
-    meta = jnp.concatenate([h_columns, x_columns], axis=1)
-    meta = jnp.pad(meta, ((0, 8 - rows_here), (0, 128 - meta.shape[1])))
     half_w = block // 2
     any_space = pl.BlockSpec(memory_space=pl.ANY)
-    smem = pl.BlockSpec(memory_space=pltpu.SMEM)
-    vmem = pl.BlockSpec(memory_space=pltpu.VMEM)
+    hbm = pl.BlockSpec(memory_space=pltpu.HBM)
     out = jax.ShapeDtypeStruct(x_blocks.shape, dtype)
     copies = 64
     return pl.pallas_call(
         functools.partial(kernel, (rows_n, cols_n, rows_here, slots, block)),
         out_shape=(out, out),
-        in_specs=[any_space, any_space, vmem, smem, smem],
+        in_specs=[hbm] * 6,
         out_specs=(any_space, any_space),
         scratch_shapes=[
-            pltpu.VMEM((rows_here + 4 * REACH + 1, 2, slots // 2, block, half_w), dtype),
+            pltpu.VMEM((rows_here + 4 * REACH - 1, 2, slots // 2, block, half_w), dtype),
+            pltpu.VMEM((4, slots // 2, block, half_w), dtype),
             pltpu.VMEM((rows_here, 2, slots // 2, block, half_w), dtype),
             pltpu.VMEM((rows_here + 2 * REACH + 1, slots, block, half_w), dtype),
             pltpu.VMEM((2, rows_here // 2, slots, block, half_w), dtype),
             pltpu.VMEM((rows_here // 2, slots, block, half_w), dtype),
-            pltpu.VMEM((3 * slots, 8, 128), jnp.int32),
-            pltpu.SMEM((3 * slots, 8, 128), jnp.int32),
+            pltpu.VMEM((slots, block, half_w), jnp.float32),
+            pltpu.VMEM((3 * slots, 1, rows_here), jnp.int32),
+            pltpu.VMEM((3,) + h_columns.shape, jnp.int32),
+            pltpu.SMEM((3 * slots, 1, rows_here), jnp.int32),
+            pltpu.SMEM((3,) + h_columns.shape, jnp.int32),
+            pltpu.SMEM(p_columns.shape, jnp.int32),
+            pltpu.SMEM(q_columns.shape, jnp.int32),
             pltpu.SemaphoreType.DMA((copies,)),
             pltpu.SemaphoreType.DMA((copies,)),
             pltpu.SemaphoreType.DMA((16,)),
         ],
         compiler_params=pltpu.CompilerParams(
-            collective_id=0, has_side_effects=True, vmem_limit_bytes=48 * 2**20
+            collective_id=0, has_side_effects=True, vmem_limit_bytes=67043328
         ),
-    )(x_blocks, h_blocks, meta, p_columns, q_columns)
+    )(x_blocks, h_blocks, x_columns.T, h_columns, p_columns, q_columns)
 
 
 def solution(mesh):

time: 60.6 us -> 52.9 us (0.87)
  Pallas kernels: 52.3 us -> 48 us
  local copies, waits for them, and re-layouts: 6.33 us -> 3.74 us
  other arithmetic: 0.75 us -> 0 us
    pallas_call x1, Pallas kernels: 52.3 us -> 48 us  [local(): pl.pallas_call(functools.partial(kernel, (rows_n, cols_n, rows_here, slot...]
    unnamed x11 -> x2, local copies, waits for them, and re-layouts: 6.32 us -> 3.74 us
    concatenate x1 -> x0, other arithmetic: 0.75 us -> none  [local(): meta = jnp.concatenate([h_columns, x_columns], axis=1)]
where the time goes in v2:
time: 52.9 us; the launch traced here: 52.3 us
  Pallas kernels  48 us (91%)
  local copies, waits for them, and re-layouts  3.74 us (7%)
  between operations  0.64 us (1%)
    pallas_call x1, Pallas kernels, local(): pl.pallas_call(functools.partial(kernel, (rows_n, cols_n, rows_here, slot...  48 us
    unnamed x2, local copies, waits for them, and re-layouts  3.74 us

profile of v2, /device:TPU:0, one launch (start us, length us, event | category | flops | bytes accessed | tf_op | source)
XLA Modules:
  0.0 52.3 jit_solution(15637043058395157320)
XLA Ops:
  0.6 48.0 %shard_map.77 = (bf16[4,1,256,256]{3,2,1,0:T(8,128)(2,1)}, bf16[4,1,256,256]{3,2,1,0:T(8,128)(2,1)}) custom-call(bf16[4,1,256,256]{3,2,1,0:T(8,128)(2,1)} %x_ref.1, bf16[4,4,256,256]{3,2,1,0:T(8,128)(2,1)} %h_ref.1, s32[1,4]{1,0:T(1,128)} %bitcast.1, s32[4,4]{1,0:T(4,128)} %hc_ref.1, s32[4,4]{1,0:T(4,128)} %pc_ref.1, s32[4,4]{1,0:T(4,128)} %qc_ref.1), custom_call_target="tpu_custom_call" | custom-call | tf_op jit(solution)/shard_map/pallas_call | solution.py:298
  48.6 1.9 %copy.10 = bf16[4,1,256,256]{3,2,1,0:T(8,128)(2,1)} copy(bf16[4,1,256,256]{3,2,1,0:T(8,128)(2,1)} %get-tuple-element.4) | data formatting | bytes 1048576
  50.5 1.9 %copy.11 = bf16[4,1,256,256]{3,2,1,0:T(8,128)(2,1)} copy(bf16[4,1,256,256]{3,2,1,0:T(8,128)(2,1)} %get-tuple-element.5) | data formatting | bytes 1048576

commit v3 on v2

--- a/solution.py
+++ b/solution.py
@@ -15,7 +15,7 @@
     sizes, x_ref, h_ref, xc_ref, hc_ref, pc_ref, qc_ref,
     out_p, out_q,
     xb, xt, xo, hb, pb, qb, qacc, xc_v, hc_v, x_cols, h_cols, p_cols, q_cols,
-    send_sem, recv_sem, local_sem,
+    send_sem, recv_sem, late_sem, local_sem,
 ):
     rows_n, cols_n, rows_here, slots, block = sizes
     groups = rows_n * cols_n
@@ -52,11 +52,12 @@
     counts = {"remote": 0, "local": 0}
     started = []
 
-    def send(src, dst, to):
+    def send(src, dst, to, landed=None):
         n = counts["remote"]
         counts["remote"] = n + 1
         copy = pltpu.make_async_remote_copy(
-            src_ref=src, dst_ref=dst, send_sem=send_sem.at[n], recv_sem=recv_sem.at[n],
+            src_ref=src, dst_ref=dst, send_sem=send_sem.at[n],
+            recv_sem=recv_sem.at[n] if landed is None else landed,
             device_id=to, device_id_type=MESH,
         )
         copy.start()
@@ -111,7 +112,7 @@
     zeros = jnp.zeros((block, half_w), hb.dtype)
     hb[hb_zero, 0] = zeros
     xb[xb_zero, 0, 0] = zeros
-    xt[3, 0] = zeros
+    xt[2, 0] = zeros
 
     local_x.wait()
     y_near.wait_recv()
@@ -122,9 +123,15 @@
             (down, down, 1), (step, wide + rows_here + step, -1)
         ):
             rim.append((send(xb.at[wide - 1 + row, c], xb.at[place - 1, c], at(to, d)), place - 1))
+    late_to = ((wide - 1, at(1, y * 2)), (wide + rows_here - 2, at(-1, y * 2 + 1)))
+    for row, to in late_to:
+        send(xb.at[row, c], xt.at[c], to, late_sem.at[c])
     late = [
-        send(xb.at[wide - 1, c], xt.at[2 * c], at(1, d)),
-        send(xb.at[wide - 1 + rows_here - 1, c], xt.at[2 - c], at(-1, d)),
+        pltpu.make_async_remote_copy(
+            src_ref=xt.at[n], dst_ref=xt.at[n], send_sem=send_sem.at[0], recv_sem=late_sem.at[n],
+            device_id=partner, device_id_type=MESH,
+        )
+        for n in range(2)
     ]
     d2d.append(send(xb.at[here, c, 1 - y], xb.at[here, c, 1 - y], partner))
     y_far.wait_recv()
@@ -259,12 +266,10 @@
     left = jnp.concatenate([pb[0, ii, pick_p], pb[1, ii, pick_p]], axis=1)
     for copy in late:
         copy.wait_recv()
-    last = send(xt.at[2], xt.at[c], partner)
-    last.wait_recv()
     for dy, dc in order + ((0, 0),):
         q = other(dy, dc)[2]
         wanted = q_cols[i, q]
-        pick_c = jnp.int32(3)
+        pick_c = jnp.int32(2)
         pick_y = jnp.int32(0)
         for m in range(slots):
             column = x_cols[2 * c * slots + m, 0, c * (rows_here - 1)]
@@ -285,6 +290,22 @@
         copy.wait_send()
 
 
+def put_out(p_ref, q_ref, p_out, q_out, p_mid, q_mid, sems):
+    pieces = p_ref.shape[0]
+    ins, outs = [], []
+    for n, (src, mid, dst) in enumerate(((p_ref, p_mid, p_out), (q_ref, q_mid, q_out))):
+        for i in range(pieces):
+            copy = pltpu.make_async_copy(src.at[i], mid.at[i], sems.at[0, n, i])
+            copy.start()
+            ins.append(copy)
+            outs.append(pltpu.make_async_copy(mid.at[i], dst.at[i], sems.at[1, n, i]))
+    for copy, out in zip(ins, outs):
+        copy.wait()
+        out.start()
+    for out in outs:
+        out.wait()
+
+
 def local(sizes, x_blocks, x_columns, h_blocks, h_columns, p_columns, q_columns):
     rows_n, cols_n = sizes
     rows_here, _, block, _ = x_blocks.shape
@@ -295,14 +316,14 @@
     hbm = pl.BlockSpec(memory_space=pltpu.HBM)
     out = jax.ShapeDtypeStruct(x_blocks.shape, dtype)
     copies = 64
-    return pl.pallas_call(
+    parts = pl.pallas_call(
         functools.partial(kernel, (rows_n, cols_n, rows_here, slots, block)),
         out_shape=(out, out),
         in_specs=[hbm] * 6,
-        out_specs=(any_space, any_space),
+        out_specs=(hbm, hbm),
         scratch_shapes=[
             pltpu.VMEM((rows_here + 4 * REACH - 1, 2, slots // 2, block, half_w), dtype),
-            pltpu.VMEM((4, slots // 2, block, half_w), dtype),
+            pltpu.VMEM((3, slots // 2, block, half_w), dtype),
             pltpu.VMEM((rows_here, 2, slots // 2, block, half_w), dtype),
             pltpu.VMEM((rows_here + 2 * REACH + 1, slots, block, half_w), dtype),
             pltpu.VMEM((2, rows_here // 2, slots, block, half_w), dtype),
@@ -316,12 +337,25 @@
             pltpu.SMEM(q_columns.shape, jnp.int32),
             pltpu.SemaphoreType.DMA((copies,)),
             pltpu.SemaphoreType.DMA((copies,)),
+            pltpu.SemaphoreType.DMA((2,)),
             pltpu.SemaphoreType.DMA((16,)),
         ],
         compiler_params=pltpu.CompilerParams(
             collective_id=0, has_side_effects=True, vmem_limit_bytes=67043328
         ),
     )(x_blocks, h_blocks, x_columns.T, h_columns, p_columns, q_columns)
+    return pl.pallas_call(
+        put_out,
+        out_shape=(out, out),
+        in_specs=[hbm] * 2,
+        out_specs=(hbm, hbm),
+        scratch_shapes=[
+            pltpu.VMEM(x_blocks.shape, dtype),
+            pltpu.VMEM(x_blocks.shape, dtype),
+            pltpu.SemaphoreType.DMA((2, 2, rows_here)),
+        ],
+        compiler_params=pltpu.CompilerParams(vmem_limit_bytes=67043328),
+    )(*parts)
 
 
 def solution(mesh):

time: 52.9 us -> 49.9 us (0.943)
  local copies, waits for them, and re-layouts: 3.74 us -> 0 us
  Pallas kernels: 48 us -> 49.1 us
    unnamed x2 -> x0, local copies, waits for them, and re-layouts: 3.74 us -> none
    pallas_call x0 -> x1, Pallas kernels: none -> 2.09 us  [local(): pl.pallas_call(put_out, out_shape=(out, out), in_specs=[hbm] * 2, out_spe...]
    pallas_call x1, Pallas kernels: 48 us -> 47 us  [local(): pl.pallas_call(functools.partial(kernel, (rows_n, cols_n, rows_here, slot...]
where the time goes in v3:
time: 49.9 us; the launch traced here: 49.7 us
  Pallas kernels  49.1 us (98%)
  between operations  0.64 us (1%)
    pallas_call x1, Pallas kernels, local(): pl.pallas_call(functools.partial(kernel, (rows_n, cols_n, rows_here, slot...  47 us
    pallas_call x1, Pallas kernels, local(): pl.pallas_call(put_out, out_shape=(out, out), in_specs=[hbm] * 2, out_spe...  2.09 us

profile of v3, /device:TPU:0, one launch (start us, length us, event | category | flops | bytes accessed | tf_op | source)
XLA Modules:
  0.0 49.7 jit_solution(14631022841827060554)
XLA Ops:
  0.6 47.0 %shard_map.77 = (bf16[4,1,256,256]{3,2,1,0:T(8,128)(2,1)}, bf16[4,1,256,256]{3,2,1,0:T(8,128)(2,1)}) custom-call(bf16[4,1,256,256]{3,2,1,0:T(8,128)(2,1)} %x_ref.1, bf16[4,4,256,256]{3,2,1,0:T(8,128)(2,1)} %h_ref.1, s32[1,4]{1,0:T(1,128)} %bitcast.1, s32[4,4]{1,0:T(4,128)} %hc_ref.1, s32[4,4]{1,0:T(4,128)} %pc_ref.1, s32[4,4]{1,0:T(4,128)} %qc_ref.1), custom_call_target="tpu_custom_call" | custom-call | tf_op jit(solution)/shard_map/pallas_call | solution.py:319
  47.6 2.1 %shard_map.78 = (bf16[4,1,256,256]{3,2,1,0:T(8,128)(2,1)}, bf16[4,1,256,256]{3,2,1,0:T(8,128)(2,1)}) custom-call(bf16[4,1,256,256]{3,2,1,0:T(8,128)(2,1)} %get-tuple-element.4.p_ref, bf16[4,1,256,256]{3,2,1,0:T(8,128)(2,1)} %get-tuple-element.5.q_ref), custom_call_target="tpu_custom_call" | custom-call | tf_op jit(solution)/shard_map/pallas_call | solution.py:347

commit v4 on v3

--- a/solution.py
+++ b/solution.py
@@ -39,15 +39,14 @@
         return yy, cc, yy * 2 + cc
 
     mates = [(0, 1), (1, 0), (1, 1)]
-    peers = [(0, dy, dc) for dy, dc in mates]
-    peers += [(s, dy, dc) for s in (1, -1) for dy in (0, 1) for dc in (0, 1)]
+    peers = [(s, dy, dc) for dy in (0, 1) for dc in (0, 1) for s in (1, -1)]
+    peers += [(0, dy, dc) for dy, dc in mates]
 
     barrier = pltpu.get_barrier_semaphore()
     for s, dy, dc in peers:
         pl.semaphore_signal(
             barrier, inc=1, device_id=at(s, other(dy, dc)[2]), device_id_type=MESH
         )
-    pl.semaphore_wait(barrier, len(peers))
 
     counts = {"remote": 0, "local": 0}
     started = []
@@ -80,6 +79,21 @@
     over = at(0, other(1, 0)[2])
     partner = at(0, other(0, 1)[2])
 
+    local_x = move(x_ref.at[:, 0, :, side(y)], xb.at[here, c, y])
+    local_o = move(x_ref.at[:, 0, :, side(1 - y)], xo.at[:, c, y])
+    local_h = move(h_ref.at[:, :, :, side(y)], hb.at[pl.ds(REACH, rows_here)])
+    pl.semaphore_wait(barrier, len(peers))
+    mine = pl.ds(c * (slots // 2), slots // 2)
+    h_up = send(
+        h_ref.at[pl.ds(rows_here - REACH, REACH), mine, :, side(y)],
+        hb.at[pl.ds(0, REACH), mine], at(1, d),
+    )
+    h_down = send(
+        h_ref.at[pl.ds(0, REACH), mine, :, side(y)],
+        hb.at[pl.ds(REACH + rows_here, REACH), mine], at(-1, d),
+    )
+    y_near = send(x_ref.at[:, 0, :, side(1 - y)], xb.at[here, c, y], over)
+
     metas = [
         send(xc_ref, xc_v.at[(1 - s) * slots + d], at(s, other(dy, dc)[2]))
         for s, dy, dc in peers
@@ -90,21 +104,7 @@
         move(pc_ref, p_cols), move(qc_ref, q_cols),
     ]
 
-    y_near = send(x_ref.at[:, 0, :, side(1 - y)], xb.at[here, c, y], over)
-    local_x = move(x_ref.at[:, 0, :, side(y)], xb.at[here, c, y])
-
-    mine = pl.ds(c * (slots // 2), slots // 2)
-    h_up = send(
-        h_ref.at[pl.ds(rows_here - REACH, REACH), mine, :, side(y)],
-        hb.at[pl.ds(0, REACH), mine], at(1, d),
-    )
-    h_down = send(
-        h_ref.at[pl.ds(0, REACH), mine, :, side(y)],
-        hb.at[pl.ds(REACH + rows_here, REACH), mine], at(-1, d),
-    )
     y_far = send(x_ref.at[:, 0, :, side(y)], xo.at[:, c, y], over)
-    local_o = move(x_ref.at[:, 0, :, side(1 - y)], xo.at[:, c, y])
-    local_h = move(h_ref.at[:, :, :, side(y)], hb.at[pl.ds(REACH, rows_here)])
     d2d = [
         send(x_ref.at[:, 0, :, side(y)], xb.at[here, c, y], partner),
         send(x_ref.at[:, 0, :, side(1 - y)], xo.at[:, c, y], partner),

time: 49.9 us -> 49.8 us (level)
  no operation moved by 1% of the time
where the time goes in v4:
time: 49.8 us; the launch traced here: 49.7 us
  Pallas kernels  49 us (98%)
  between operations  0.64 us (1%)
    pallas_call x1, Pallas kernels, local(): pl.pallas_call(functools.partial(kernel, (rows_n, cols_n, rows_here, slot...  46.9 us
    pallas_call x1, Pallas kernels, local(): pl.pallas_call(put_out, out_shape=(out, out), in_specs=[hbm] * 2, out_spe...  2.09 us

profile of v4, /device:TPU:0, one launch (start us, length us, event | category | flops | bytes accessed | tf_op | source)
XLA Modules:
  0.0 49.7 jit_solution(2172609164037503796)
XLA Ops:
  0.6 46.9 %shard_map.77 = (bf16[4,1,256,256]{3,2,1,0:T(8,128)(2,1)}, bf16[4,1,256,256]{3,2,1,0:T(8,128)(2,1)}) custom-call(bf16[4,1,256,256]{3,2,1,0:T(8,128)(2,1)} %x_ref.1, bf16[4,4,256,256]{3,2,1,0:T(8,128)(2,1)} %h_ref.1, s32[1,4]{1,0:T(1,128)} %bitcast.1, s32[4,4]{1,0:T(4,128)} %hc_ref.1, s32[4,4]{1,0:T(4,128)} %pc_ref.1, s32[4,4]{1,0:T(4,128)} %qc_ref.1), custom_call_target="tpu_custom_call" | custom-call | tf_op jit(solution)/shard_map/pallas_call | solution.py:319
  47.6 2.1 %shard_map.78 = (bf16[4,1,256,256]{3,2,1,0:T(8,128)(2,1)}, bf16[4,1,256,256]{3,2,1,0:T(8,128)(2,1)}) custom-call(bf16[4,1,256,256]{3,2,1,0:T(8,128)(2,1)} %get-tuple-element.4.p_ref, bf16[4,1,256,256]{3,2,1,0:T(8,128)(2,1)} %get-tuple-element.5.q_ref), custom_call_target="tpu_custom_call" | custom-call | tf_op jit(solution)/shard_map/pallas_call | solution.py:347

commit v5 on v4

--- a/solution.py
+++ b/solution.py
@@ -291,14 +291,16 @@
 
 
 def put_out(p_ref, q_ref, p_out, q_out, p_mid, q_mid, sems):
-    pieces = p_ref.shape[0]
+    pieces = 2
+    span = p_ref.shape[0] // pieces
+    at = lambda ref, i: ref.at[pl.ds(i * span, span)]
     ins, outs = [], []
     for n, (src, mid, dst) in enumerate(((p_ref, p_mid, p_out), (q_ref, q_mid, q_out))):
         for i in range(pieces):
-            copy = pltpu.make_async_copy(src.at[i], mid.at[i], sems.at[0, n, i])
+            copy = pltpu.make_async_copy(at(src, i), at(mid, i), sems.at[0, n, i])
             copy.start()
             ins.append(copy)
-            outs.append(pltpu.make_async_copy(mid.at[i], dst.at[i], sems.at[1, n, i]))
+            outs.append(pltpu.make_async_copy(at(mid, i), at(dst, i), sems.at[1, n, i]))
     for copy, out in zip(ins, outs):
         copy.wait()
         out.start()

time: 49.8 us -> 49.8 us (level)
  no operation moved by 1% of the time
where the time goes in v5:
time: 49.8 us; the launch traced here: 49.6 us
  Pallas kernels  49 us (98%)
  between operations  0.64 us (1%)
    pallas_call x1, Pallas kernels, local(): pl.pallas_call(functools.partial(kernel, (rows_n, cols_n, rows_here, slot...  46.9 us
    pallas_call x1, Pallas kernels, local(): pl.pallas_call(put_out, out_shape=(out, out), in_specs=[hbm] * 2, out_spe...  2.05 us

profile of v5, /device:TPU:0, one launch (start us, length us, event | category | flops | bytes accessed | tf_op | source)
XLA Modules:
  0.0 49.6 jit_solution(8691636179113903653)
XLA Ops:
  0.6 46.9 %shard_map.77 = (bf16[4,1,256,256]{3,2,1,0:T(8,128)(2,1)}, bf16[4,1,256,256]{3,2,1,0:T(8,128)(2,1)}) custom-call(bf16[4,1,256,256]{3,2,1,0:T(8,128)(2,1)} %x_ref.1, bf16[4,4,256,256]{3,2,1,0:T(8,128)(2,1)} %h_ref.1, s32[1,4]{1,0:T(1,128)} %bitcast.1, s32[4,4]{1,0:T(4,128)} %hc_ref.1, s32[4,4]{1,0:T(4,128)} %pc_ref.1, s32[4,4]{1,0:T(4,128)} %qc_ref.1), custom_call_target="tpu_custom_call" | custom-call | tf_op jit(solution)/shard_map/pallas_call | solution.py:321
  47.6 2.1 %shard_map.78 = (bf16[4,1,256,256]{3,2,1,0:T(8,128)(2,1)}, bf16[4,1,256,256]{3,2,1,0:T(8,128)(2,1)}) custom-call(bf16[4,1,256,256]{3,2,1,0:T(8,128)(2,1)} %get-tuple-element.4.p_ref, bf16[4,1,256,256]{3,2,1,0:T(8,128)(2,1)} %get-tuple-element.5.q_ref), custom_call_target="tpu_custom_call" | custom-call | tf_op jit(solution)/shard_map/pallas_call | solution.py:349
